TPU v7x, 256 devices: a whole 4x4x8 slice. The times are simulated.
256 devices in a mesh: dp: 16 (over z, core), tensor: 4 (over y), corpus: 4 (over x).
Axes of the slice: x: 4, y: 4, z: 8, core: 2. Of those that a mesh axis runs over, the one named last changes fastest.
Arguments:
- queries: bfloat16 [4096, 2048], P(('dp', 'tensor', 'corpus')), may hold values from -24 to 24
- passages: bfloat16 [65536, 2048], P(('dp', 'corpus'), 'tensor'), may hold values from -6 to 6
- pos_ids: int32 [4096], P(('dp', 'tensor', 'corpus')), may hold values from 0 to 65535, as said below
- neg_ids: int32 [4096, 32], P(('dp', 'tensor', 'corpus')), may hold values from 0 to 65535, as said below
Outputs:
- grad_query: float32 [4096, 2048], P(('dp', 'tensor', 'corpus'))
- losses: float32 [4096], P(('dp', 'tensor', 'corpus'))
- grad_pass: float32 [65536, 2048], P(('dp', 'corpus'), 'tensor')
Inputs may be any that keep to these rules, and one draw needn't show every extreme that they name: `pos_ids`: together with neg_ids: the ids named by the 16 queries of one device, positives and negatives together, fall at most 16 times into one block of 1024 passage rows (rows b * 1024 to (b + 1) * 1024 - 1), and exactly 16 times into one block that is the same for every device. Ids may repeat. `neg_ids`: counted together with pos_ids as stated there.
All inputs are finite; a program needn't handle non-finite values.
Results may differ from a plain program's by a relative error of at most 0.0035.
Values may be sent and summed in bfloat16 or wider, within the bound.
A program may use at most 128 MiB of HBM per device.

v0:
```python
import jax
import jax.numpy as jnp
from jax import lax
from jax.sharding import PartitionSpec as P


def lookup_rows(row_table, asked_ids):
    return jnp.take(row_table, asked_ids, axis=0, mode="fill", fill_value=0)


def body(queries, passages, pos_ids, neg_ids):
    per_device, feat_width = queries.shape
    block_rows, shard_width = passages.shape
    neg_count = neg_ids.shape[1]
    owners = lax.axis_size("dp") * lax.axis_size("corpus")
    slot_count = 2 * per_device * (neg_count + 1) // owners
    score_scale = feat_width ** (-0.5)
    wanted = jnp.concatenate([pos_ids[:, None], neg_ids], axis=1).reshape(-1)
    owner_of = wanted // block_rows
    local_row = wanted % block_rows
    matches = (owner_of[:, None] == jnp.arange(owners)[None, :]).astype(jnp.int32)
    earlier = jnp.cumsum(matches, axis=0) - matches
    slot_of = owner_of * slot_count + jnp.sum(earlier * matches, axis=1)
    send_ids = jnp.full((owners * slot_count,), block_rows, jnp.int32).at[slot_of].set(local_row)
    send_ids = send_ids.reshape(owners, slot_count)
    row_table = lax.all_gather(passages, "tensor", axis=1, tiled=True)
    asked_ids = lax.all_to_all(send_ids, ("dp", "corpus"), split_axis=0, concat_axis=0, tiled=True)
    found = lookup_rows(row_table, asked_ids)
    fetched = lax.all_to_all(found, ("dp", "corpus"), split_axis=0, concat_axis=0, tiled=True)
    gathered = fetched.reshape(owners * slot_count, feat_width)[slot_of]
    gathered = gathered.reshape(per_device, neg_count + 1, feat_width)
    pos_rows = gathered[:, 0, :]
    neg_rows = gathered[:, 1:, :]
    in_batch = lax.all_gather(pos_rows, "dp", axis=0, tiled=True)
    columns = in_batch.shape[0]
    in_scores = (
        lax.dot_general(
            queries, in_batch, (((1,), (1,)), ((), ())), preferred_element_type=jnp.float32
        )
        * score_scale
    )
    neg_scores = (
        jnp.einsum("md,mkd->mk", queries, neg_rows, preferred_element_type=jnp.float32)
        * score_scale
    )
    logits = jnp.concatenate([in_scores, neg_scores], axis=1)
    row_max = jnp.max(logits, axis=1, keepdims=True)
    exponent = jnp.exp(logits - row_max)
    denominator = jnp.sum(exponent, axis=1, keepdims=True)
    own_col = lax.axis_index("dp") * per_device + jnp.arange(per_device)
    target = (jnp.arange(columns + neg_count)[None, :] == own_col[:, None]).astype(jnp.float32)
    losses = jnp.log(denominator[:, 0]) + row_max[:, 0] - jnp.sum(target * logits, axis=1)
    weights = (exponent / denominator - target).astype(jnp.bfloat16)
    in_weights = weights[:, :columns]
    neg_weights = weights[:, columns:]
    grad_query = jnp.dot(in_weights, in_batch, preferred_element_type=jnp.float32)
    grad_query = grad_query + jnp.einsum(
        "mk,mkd->md", neg_weights, neg_rows, preferred_element_type=jnp.float32
    )
    grad_query = grad_query * score_scale
    in_terms = lax.dot_general(
        in_weights, queries, (((0,), (0,)), ((), ())), preferred_element_type=jnp.float32
    )
    pos_grad = lax.psum_scatter(in_terms, "dp", scatter_dimension=0, tiled=True) * score_scale
    neg_grad = (
        neg_weights.astype(jnp.float32)[:, :, None]
        * queries.astype(jnp.float32)[:, None, :]
        * score_scale
    )
    row_grads = jnp.concatenate([pos_grad[:, None, :], neg_grad], axis=1).astype(jnp.bfloat16)
    row_grads = row_grads.reshape(-1, feat_width)
    grad_slots = (
        jnp.zeros((owners * slot_count, feat_width), jnp.bfloat16).at[slot_of].set(row_grads)
    )
    grad_slots = grad_slots.reshape(owners, slot_count, feat_width)
    arrived = lax.all_to_all(grad_slots, ("dp", "corpus"), split_axis=0, concat_axis=0, tiled=True)
    accum_grad = jnp.zeros((block_rows, feat_width), jnp.float32)
    accum_grad = accum_grad.at[asked_ids.reshape(-1)].add(
        arrived.reshape(-1, feat_width).astype(jnp.float32), mode="drop"
    )
    grad_pass = lax.psum_scatter(accum_grad, "tensor", scatter_dimension=1, tiled=True)
    return (grad_query, losses, grad_pass)


def solution(mesh):
    in_specs = (
        P(("dp", "tensor", "corpus"), None),
        P(("dp", "corpus"), "tensor"),
        P(("dp", "tensor", "corpus")),
        P(("dp", "tensor", "corpus"), None),
    )
    out_specs = (
        P(("dp", "tensor", "corpus"), None),
        P(("dp", "tensor", "corpus")),
        P(("dp", "corpus"), "tensor"),
    )
    return jax.shard_map(body, mesh=mesh, in_specs=in_specs, out_specs=out_specs, check_vma=False)
```

profile of v0, /device:TPU:1, one launch (start us, length us, event | category | flops | bytes accessed | tf_op | source)
XLA Modules:
  0.0 520.4 jit_solution(17081883421997860384)
XLA Ops:
  9.7 1.5 reduce-window.6
  11.7 4.1 scatter_custom_fusion
  15.8 22.0 %all_to_all.25 = s32[64,1,16]{2,1,0:T(1,128)S(1)} all-to-all(s32[64,1,16]{2,1,0:T(1,128)S(1)} %bitcast.53), channel_id=1, replica_groups=mesh['dp'=16,'tensor'=4,'corpus'=4] {'dp','corpus'}, dimensions={0} | all-to-all | bytes 8192 | tf_op jit(solution)/shard_map/all_to_all | solution.py:27
  37.9 26.3 %all-gather.4.cloned.1.call-done = bf16[1024,2048]{1,0:T(8,128)(2,1)} async-done(((bf16[1024,512]{1,0:T(8,128)(2,1)}), bf16[1024,2048]{1,0:T(8,128)(2,1)}) %all-gather.4.cloned.1.call-update) | async-done | bytes 4194320 | tf_op jit(solution)/shard_map/all_gather | solution.py:26
  64.2 11.6 %gather_fusion = bf16[1024,2048]{1,0:T(8,128)(2,1)} fusion(bf16[1024,2048]{1,0:T(8,128)(2,1)} %all-gather.4.cloned.1.call-done, s32[1024]{0:T(1024)S(1)} %broadcast_clamp_fusion), kind=kCustom, calls=%fused_computation | custom fusion | bytes 8392704 | tf_op jit(solution)/shard_map/jit(_take)/gather | solution.py:8
  75.8 4.5 broadcast_select_fusion
  80.3 11.0 %all-to-all-start.1 = ((bf16[64,16,2048]{2,1,0:T(8,128)(2,1)}), bf16[64,16,2048]{2,1,0:T(8,128)(2,1)}, u32[]{:S(2)}, u32[]{:S(2)}) async-start(bf16[64,16,2048]{2,1,0:T(8,128)(2,1)} %broadcast_select_fusion), calls=%async_computation.1 | async-start | bytes 8388608 | tf_op jit(solution)/shard_map/all_to_all | solution.py:29
  91.4 93.5 %all-to-all-done.1 = bf16[64,16,2048]{2,1,0:T(8,128)(2,1)} async-done(((bf16[64,16,2048]{2,1,0:T(8,128)(2,1)}), bf16[64,16,2048]{2,1,0:T(8,128)(2,1)}, u32[]{:S(2)}, u32[]{:S(2)}) %all-to-all-start.1) | async-done | bytes 4194336 | tf_op jit(solution)/shard_map/all_to_all | solution.py:29
  184.9 9.0 %gather_fusion.1 = bf16[528,2048]{1,0:T(8,128)(2,1)S(1)} fusion(bf16[1024,2048]{1,0:T(8,128)(2,1)} %bitcast.6, s32[1024]{0:T(1024)S(1)} %pad_clamp_fusion), kind=kCustom, calls=%fused_computation.1 | custom fusion | bytes 4327488 | tf_op jit(solution)/shard_map/gather | solution.py:30
  193.9 1.9 reshape.222
  197.8 2.4 fusion.8
  200.4 34.0 %all-gather.6.cloned.1.call-done = bf16[256,1,2048]{2,0,1:T(8,128)(2,1)} async-done(((bf16[16,1,2048]{2,0,1:T(8,128)(2,1)}), bf16[256,1,2048]{2,0,1:T(8,128)(2,1)}) %all-gather.6.cloned.1.call-update) | async-done | bytes 1048592 | tf_op jit(solution)/shard_map/all_gather | solution.py:34
  234.4 1.7 fusion.27
  236.4 1.8 fusion.18
  238.2 1.8 multiply_convert_fusion
  240.1 53.7 %reduce-scatter.3.cloned.1.call-done = f32[16,2048]{1,0:T(8,128)} async-done(((f32[256,2048]{1,0:T(8,128)}), f32[16,2048]{1,0:T(8,128)}) %reduce-scatter.3.cloned.1.call-update) | async-done | bytes 131088 | tf_op jit(solution)/shard_map/reduce_scatter | solution.py:64
  294.8 2.4 pad_maximum_fusion
  297.2 1.8 reshape.255
  299.0 10.4 %scatter_custom_fusion.1 = bf16[1024,2048]{1,0:T(8,128)(2,1)} fusion(s32[528]{0:T(1024)S(1)} %fusion.23, bf16[528,2048]{1,0:T(8,128)(2,1)} %reshape.255, bf16[]{:T(256)} %constant.66.clone.1), kind=kCustom, calls=%fused_computation.13 | custom fusion | bytes 4194816 | tf_op jit(solution)/shard_map/scatter | solution.py:73
  309.4 10.7 %all-to-all-start.2 = ((bf16[64,16,2048]{2,1,0:T(8,128)(2,1)}), bf16[64,16,2048]{2,1,0:T(8,128)(2,1)}, u32[]{:S(2)}, u32[]{:S(2)}) async-start(bf16[64,16,2048]{2,1,0:T(8,128)(2,1)} %bitcast.46), calls=%async_computation.3 | async-start | bytes 8388608 | tf_op jit(solution)/shard_map/all_to_all | solution.py:76
  321.7 91.9 %all-to-all-done.2 = bf16[64,16,2048]{2,1,0:T(8,128)(2,1)} async-done(((bf16[64,16,2048]{2,1,0:T(8,128)(2,1)}), bf16[64,16,2048]{2,1,0:T(8,128)(2,1)}, u32[]{:S(2)}, u32[]{:S(2)}) %all-to-all-start.2) | async-done | bytes 4194336 | tf_op jit(solution)/shard_map/all_to_all | solution.py:76
  413.7 18.3 %scatter_custom_fusion.2 = f32[1024,2048]{1,0:T(8,128)} fusion(s32[1024]{0:T(1024)S(1)} %bitcast.56, bf16[1024,2048]{1,0:T(8,128)(2,1)} %bitcast.18, f32[]{:T(128)} %constant.69.clone.1), kind=kCustom, calls=%fused_computation.5 | custom fusion | flops 4194304 | bytes 12582916 | tf_op jit(solution)/shard_map/scatter-add | solution.py:78
  432.6 2.4 fusion.6
  435.8 78.0 %reduce-scatter.5.cloned.1.call-done = f32[1024,512]{1,0:T(8,128)} async-done(((f32[1024,2048]{1,0:T(8,128)}), f32[1024,512]{1,0:T(8,128)}) %reduce-scatter.5.cloned.1.call-update) | async-done | bytes 2097168 | tf_op jit(solution)/shard_map/reduce_scatter | solution.py:81
  (47 shorter events, 9.7 us)
Async XLA Ops:
  7.2 57.1 %all-gather.4.cloned.1.call-start = ((), (), s32[]{:S(2)}) async-start(), calls=%async_computation.5 | async-start | bytes 5242880 | tf_op jit(solution)/shard_map/all_gather | solution.py:26
  80.3 104.6 %all-to-all-start.1 = ((bf16[64,16,2048]{2,1,0:T(8,128)(2,1)}), bf16[64,16,2048]{2,1,0:T(8,128)(2,1)}, u32[]{:S(2)}, u32[]{:S(2)}) async-start(bf16[64,16,2048]{2,1,0:T(8,128)(2,1)} %broadcast_select_fusion), calls=%async_computation.1 | async-start | bytes 8388608 | tf_op jit(solution)/shard_map/all_to_all | solution.py:29
  91.3 143.0 %all-gather.6.cloned.1.call-start = ((), (), s32[]{:S(2)}) async-start(), calls=%async_computation.8 | async-start | bytes 1114112 | tf_op jit(solution)/shard_map/all_gather | solution.py:34
  193.9 3.9 copy-start.1
  197.6 96.2 %reduce-scatter.3.cloned.1.call-start = ((), (), s32[]{:S(2)}) async-start(), calls=%async_computation.6 | async-start | bytes 2228224 | tf_op jit(solution)/shard_map/reduce_scatter | solution.py:64
  309.4 104.3 %all-to-all-start.2 = ((bf16[64,16,2048]{2,1,0:T(8,128)(2,1)}), bf16[64,16,2048]{2,1,0:T(8,128)(2,1)}, u32[]{:S(2)}, u32[]{:S(2)}) async-start(bf16[64,16,2048]{2,1,0:T(8,128)(2,1)} %bitcast.46), calls=%async_computation.3 | async-start | bytes 8388608 | tf_op jit(solution)/shard_map/all_to_all | solution.py:76
  320.1 193.7 %reduce-scatter.5.cloned.1.call-start = ((), (), s32[]{:S(2)}) async-start(), calls=%async_computation.7 | async-start | bytes 10485760 | tf_op jit(solution)/shard_map/reduce_scatter | solution.py:81
  432.0 2.9 copy-start
Sparse Core Ops, SparseCore 0:
  9.8 54.3 all-gather.3
  197.7 36.6 all-gather.5
  238.3 55.4 reduce-scatter.2
  432.2 81.6 reduce-scatter.4
where the time goes:
time: 521 us; the launch traced here: 520 us
  waiting for transfers between devices  378 us (73%)
  local copies, waits for them, and re-layouts  42.5 us (8%)
  other arithmetic  32.2 us (6%)
  starting transfers between devices  22.3 us (4%)
  blocking collectives  22 us (4%)
  between operations  14 us (3%)
  matrix products  9.2 us (2%)
    all_to_all x1, waiting for transfers between devices, body(): lax.all_to_all(found, ('dp', 'corpus'), split_axis=0, concat_axis=0, tile...  93.5 us
    all_to_all x1, waiting for transfers between devices, body(): lax.all_to_all(grad_slots, ('dp', 'corpus'), split_axis=0, concat_axis=0,...  91.9 us
    reduce_scatter x1, waiting for transfers between devices, body(): lax.psum_scatter(accum_grad, 'tensor', scatter_dimension=1, tiled=True)  78 us
    reduce_scatter x1, waiting for transfers between devices, body(): lax.psum_scatter(in_terms, 'dp', scatter_dimension=0, tiled=True)  53.7 us
    all_gather x1, waiting for transfers between devices, body(): in_batch = lax.all_gather(pos_rows, 'dp', axis=0, tiled=True)  34 us
    all_gather x1, waiting for transfers between devices, body(): row_table = lax.all_gather(passages, 'tensor', axis=1, tiled=True)  26.3 us
    all_to_all x1, blocking collectives, body(): lax.all_to_all(send_ids, ('dp', 'corpus'), split_axis=0, concat_axis=0, t...  22 us
    scatter-add x1, other arithmetic, body(): accum_grad.at[asked_ids.reshape(-1)]  18.3 us
  transfers between devices with their start and end apart: 6, of which 6 were waited for; matrix products, arithmetic and copies ran while one was open for 3% of the time, Pallas kernels for 0%

commit v1 on v0

--- a/solution.py
+++ b/solution.py
@@ -23,7 +23,9 @@
     slot_of = owner_of * slot_count + jnp.sum(earlier * matches, axis=1)
     send_ids = jnp.full((owners * slot_count,), block_rows, jnp.int32).at[slot_of].set(local_row)
     send_ids = send_ids.reshape(owners, slot_count)
-    row_table = lax.all_gather(passages, "tensor", axis=1, tiled=True)
+    row_table = jnp.concatenate(
+        lax.all_to_all(jnp.stack([passages] * lax.axis_size("tensor")), "tensor", 0, 0), axis=1
+    )
     asked_ids = lax.all_to_all(send_ids, ("dp", "corpus"), split_axis=0, concat_axis=0, tiled=True)
     found = lookup_rows(row_table, asked_ids)
     fetched = lax.all_to_all(found, ("dp", "corpus"), split_axis=0, concat_axis=0, tiled=True)

time: 521 us -> 550 us (1.056)
  waiting for transfers between devices: 378 us -> 398 us
  local copies, waits for them, and re-layouts: 42.5 us -> 50.8 us
    all_to_all x0 -> x1, waiting for transfers between devices: none -> 47.9 us  [body(): lax.all_to_all(jnp.stack([passages] * lax.axis_size('tensor')), 'tensor',...]
    all_gather x1 -> x0, waiting for transfers between devices: 26.3 us -> none  [body(): row_table = lax.all_gather(passages, 'tensor', axis=1, tiled=True)]
  transfers between devices with their start and end apart: 6 -> 6, of which waited for: 6 -> 6; matrix products, arithmetic and copies ran while one was open for 3% -> 2% of each run, Pallas kernels for 0% -> 0%
where the time goes in v1:
time: 550 us; the launch traced here: 549 us
  waiting for transfers between devices  398 us (72%)
  local copies, waits for them, and re-layouts  50.8 us (9%)
  other arithmetic  32.2 us (6%)
  starting transfers between devices  23 us (4%)
  blocking collectives  22 us (4%)
  between operations  14 us (3%)
  matrix products  9.2 us (2%)
    all_to_all x1, waiting for transfers between devices, body(): lax.all_to_all(found, ('dp', 'corpus'), split_axis=0, concat_axis=0, tile...  93.5 us
    all_to_all x1, waiting for transfers between devices, body(): lax.all_to_all(grad_slots, ('dp', 'corpus'), split_axis=0, concat_axis=0,...  91.9 us
    reduce_scatter x1, waiting for transfers between devices, body(): lax.psum_scatter(accum_grad, 'tensor', scatter_dimension=1, tiled=True)  78 us
    reduce_scatter x1, waiting for transfers between devices, body(): lax.psum_scatter(in_terms, 'dp', scatter_dimension=0, tiled=True)  53.7 us
    all_to_all x1, waiting for transfers between devices, body(): lax.all_to_all(jnp.stack([passages] * lax.axis_size('tensor')), 'tensor',...  47.9 us
    all_gather x1, waiting for transfers between devices, body(): in_batch = lax.all_gather(pos_rows, 'dp', axis=0, tiled=True)  33.2 us
    all_to_all x1, blocking collectives, body(): lax.all_to_all(send_ids, ('dp', 'corpus'), split_axis=0, concat_axis=0, t...  22 us
    scatter-add x1, other arithmetic, body(): accum_grad.at[asked_ids.reshape(-1)]  18.3 us
  transfers between devices with their start and end apart: 6, of which 6 were waited for; matrix products, arithmetic and copies ran while one was open for 2% of the time, Pallas kernels for 0%

profile of v1, /device:TPU:1, one launch (start us, length us, event | category | flops | bytes accessed | tf_op | source)
XLA Modules:
  0.0 549.5 jit_solution(5015490743933873131)
XLA Ops:
  10.9 4.1 scatter_custom_fusion
  15.1 22.0 %all_to_all.30 = s32[64,1,16]{2,1,0:T(1,128)S(1)} all-to-all(s32[64,1,16]{2,1,0:T(1,128)S(1)} %bitcast.57), channel_id=1, replica_groups=mesh['dp'=16,'tensor'=4,'corpus'=4] {'dp','corpus'}, dimensions={0} | all-to-all | bytes 8192 | tf_op jit(solution)/shard_map/all_to_all | solution.py:29
  37.1 3.5 stack.2
  40.6 4.9 all-to-all-start.1
  45.6 47.9 %all-to-all-done.1 = bf16[4,1024,512]{2,1,0:T(8,128)(2,1)} async-done(((bf16[4,1024,512]{2,1,0:T(8,128)(2,1)}), bf16[4,1024,512]{2,1,0:T(8,128)(2,1)}, u32[]{:S(2)}, u32[]{:S(2)}) %all-to-all-start.1) | async-done | bytes 4194336 | tf_op jit(solution)/shard_map/all_to_all | solution.py:27
  93.5 4.8 copy.26
  98.3 11.6 %gather_fusion = bf16[1024,2048]{1,0:T(8,128)(2,1)} fusion(bf16[1024,2048]{1,0:T(8,128)(2,1)} %bitcast.49, s32[1024]{0:T(1024)S(1)} %broadcast_clamp_fusion), kind=kCustom, calls=%fused_computation | custom fusion | bytes 8392704 | tf_op jit(solution)/shard_map/jit(_take)/gather | solution.py:8
  109.8 4.5 broadcast_select_fusion
  114.3 6.8 %all-to-all-start.2 = ((bf16[64,16,2048]{2,1,0:T(8,128)(2,1)}), bf16[64,16,2048]{2,1,0:T(8,128)(2,1)}, u32[]{:S(2)}, u32[]{:S(2)}) async-start(bf16[64,16,2048]{2,1,0:T(8,128)(2,1)} %broadcast_select_fusion), calls=%async_computation.2 | async-start | bytes 8388608 | tf_op jit(solution)/shard_map/all_to_all | solution.py:31
  121.3 93.5 %all-to-all-done.2 = bf16[64,16,2048]{2,1,0:T(8,128)(2,1)} async-done(((bf16[64,16,2048]{2,1,0:T(8,128)(2,1)}), bf16[64,16,2048]{2,1,0:T(8,128)(2,1)}, u32[]{:S(2)}, u32[]{:S(2)}) %all-to-all-start.2) | async-done | bytes 4194336 | tf_op jit(solution)/shard_map/all_to_all | solution.py:31
  214.8 9.0 %gather_fusion.1 = bf16[528,2048]{1,0:T(8,128)(2,1)S(1)} fusion(bf16[1024,2048]{1,0:T(8,128)(2,1)} %bitcast.7, s32[1024]{0:T(1024)S(1)} %pad_clamp_fusion), kind=kCustom, calls=%fused_computation.1 | custom fusion | bytes 4327488 | tf_op jit(solution)/shard_map/gather | solution.py:32
  223.8 1.9 reshape.232
  227.8 2.4 fusion.8
  230.3 33.2 %all-gather.3.cloned.1.call-done = bf16[256,1,2048]{2,0,1:T(8,128)(2,1)} async-done(((bf16[16,1,2048]{2,0,1:T(8,128)(2,1)}), bf16[256,1,2048]{2,0,1:T(8,128)(2,1)}) %all-gather.3.cloned.1.call-update) | async-done | bytes 1048592 | tf_op jit(solution)/shard_map/all_gather | solution.py:36
  265.5 1.8 fusion.18
  267.3 1.8 multiply_convert_fusion
  269.1 53.7 %reduce-scatter.3.cloned.1.call-done = f32[16,2048]{1,0:T(8,128)} async-done(((f32[256,2048]{1,0:T(8,128)}), f32[16,2048]{1,0:T(8,128)}) %reduce-scatter.3.cloned.1.call-update) | async-done | bytes 131088 | tf_op jit(solution)/shard_map/reduce_scatter | solution.py:66
  323.9 2.4 pad_maximum_fusion
  328.0 10.4 %scatter_custom_fusion.1 = bf16[1024,2048]{1,0:T(8,128)(2,1)} fusion(s32[528]{0:T(1024)S(1)} %fusion.23, bf16[528,2048]{1,0:T(8,128)(2,1)} %reshape.265, bf16[]{:T(256)} %constant.66.clone.1), kind=kCustom, calls=%fused_computation.13 | custom fusion | bytes 4194816 | tf_op jit(solution)/shard_map/scatter | solution.py:75
  338.4 10.8 %all-to-all-start.3 = ((bf16[64,16,2048]{2,1,0:T(8,128)(2,1)}), bf16[64,16,2048]{2,1,0:T(8,128)(2,1)}, u32[]{:S(2)}, u32[]{:S(2)}) async-start(bf16[64,16,2048]{2,1,0:T(8,128)(2,1)} %bitcast.50), calls=%async_computation.4 | async-start | bytes 8388608 | tf_op jit(solution)/shard_map/all_to_all | solution.py:78
  350.8 91.9 %all-to-all-done.3 = bf16[64,16,2048]{2,1,0:T(8,128)(2,1)} async-done(((bf16[64,16,2048]{2,1,0:T(8,128)(2,1)}), bf16[64,16,2048]{2,1,0:T(8,128)(2,1)}, u32[]{:S(2)}, u32[]{:S(2)}) %all-to-all-start.3) | async-done | bytes 4194336 | tf_op jit(solution)/shard_map/all_to_all | solution.py:78
  442.7 18.3 %scatter_custom_fusion.2 = f32[1024,2048]{1,0:T(8,128)} fusion(s32[1024]{0:T(1024)S(1)} %bitcast.60, bf16[1024,2048]{1,0:T(8,128)(2,1)} %bitcast.19, f32[]{:T(128)} %constant.69.clone.1), kind=kCustom, calls=%fused_computation.5 | custom fusion | flops 4194304 | bytes 12582916 | tf_op jit(solution)/shard_map/scatter-add | solution.py:80
  461.6 2.4 fusion.6
  464.9 78.0 %reduce-scatter.5.cloned.1.call-done = f32[1024,512]{1,0:T(8,128)} async-done(((f32[1024,2048]{1,0:T(8,128)}), f32[1024,512]{1,0:T(8,128)}) %reduce-scatter.5.cloned.1.call-update) | async-done | bytes 2097168 | tf_op jit(solution)/shard_map/reduce_scatter | solution.py:83
  (48 shorter events, 13.9 us)
Async XLA Ops:
  40.6 52.9 %all-to-all-start.1 = ((bf16[4,1024,512]{2,1,0:T(8,128)(2,1)}), bf16[4,1024,512]{2,1,0:T(8,128)(2,1)}, u32[]{:S(2)}, u32[]{:S(2)}) async-start(bf16[4,1024,512]{2,1,0:T(8,128)(2,1)} %stack.2), calls=%async_computation.1 | async-start | bytes 8388608 | tf_op jit(solution)/shard_map/all_to_all | solution.py:27
  114.3 100.4 %all-to-all-start.2 = ((bf16[64,16,2048]{2,1,0:T(8,128)(2,1)}), bf16[64,16,2048]{2,1,0:T(8,128)(2,1)}, u32[]{:S(2)}, u32[]{:S(2)}) async-start(bf16[64,16,2048]{2,1,0:T(8,128)(2,1)} %broadcast_select_fusion), calls=%async_computation.2 | async-start | bytes 8388608 | tf_op jit(solution)/shard_map/all_to_all | solution.py:31
  121.2 142.2 %all-gather.3.cloned.1.call-start = ((), (), s32[]{:S(2)}) async-start(), calls=%async_computation.8 | async-start | bytes 1114112 | tf_op jit(solution)/shard_map/all_gather | solution.py:36
  223.8 3.9 copy-start.1
  227.5 95.3 %reduce-scatter.3.cloned.1.call-start = ((), (), s32[]{:S(2)}) async-start(), calls=%async_computation.6 | async-start | bytes 2228224 | tf_op jit(solution)/shard_map/reduce_scatter | solution.py:66
  338.4 104.3 %all-to-all-start.3 = ((bf16[64,16,2048]{2,1,0:T(8,128)(2,1)}), bf16[64,16,2048]{2,1,0:T(8,128)(2,1)}, u32[]{:S(2)}, u32[]{:S(2)}) async-start(bf16[64,16,2048]{2,1,0:T(8,128)(2,1)} %bitcast.50), calls=%async_computation.4 | async-start | bytes 8388608 | tf_op jit(solution)/shard_map/all_to_all | solution.py:78
  349.2 193.7 %reduce-scatter.5.cloned.1.call-start = ((), (), s32[]{:S(2)}) async-start(), calls=%async_computation.7 | async-start | bytes 10485760 | tf_op jit(solution)/shard_map/reduce_scatter | solution.py:83
  461.1 2.9 copy-start
Sparse Core Ops, SparseCore 0:
  227.6 35.7 all-gather.2
  267.4 55.3 reduce-scatter.2
  461.2 81.6 reduce-scatter.4
